TPU v7x, 256 devices: a whole 4x4x8 slice. The times are simulated.
256 devices in a mesh: seg: 8 (over x, y_hi), gx: 2 (over y_lo), gz: 16 (over z, core).
Axes of the slice: x: 4, y: 4 (y_hi: 2, y_lo: 2; y = y_hi * 2 + y_lo), z: 8, core: 2. Of those that a mesh axis runs over, the one named last changes fastest.
Arguments:
- terminal: float32 [8, 3, 128, 256, 256], P('seg', None, 'gx', 'gz'), may hold values from -6 to 6
- jump: float32 [8, 3, 128, 256, 256], P('seg', None, 'gx', 'gz'), may hold values from -61 to 61
- tangent: float32 [8, 3, 128, 256, 256], P('seg', None, 'gx', 'gz'), may hold values from -36 to 36
- base_velocity: float32 [256], replicated, may hold values from 0.5 to 2
- base_shear: float32 [256], replicated, may hold values from -2 to 2
Outputs:
- adjoint_field: float32 [8, 3, 128, 256, 256], P('seg', None, 'gx', 'gz')
All inputs are finite; a program needn't handle non-finite values. Where the computation divides by a largest or mean magnitude, that divisor is 1e-20 or more.
Results may differ from a plain program's by a relative error of at most 0.00018.
Values sent between devices are 32-bit elements; how exact they have to be, the bound alone decides.
A program may use at most 64 MiB of HBM per device.

v0:
```python
import jax
import jax.numpy as jnp
import numpy as np
from jax import lax
from jax.sharding import PartitionSpec as P

STEPS = 4
TIME_STEP = 0.15
DIFFUSE = 0.1
WALL_COEF = 0.0002
EPSILON = 1e-06
NEWTON_TURNS = 100


def with_halo(cells, sides, width):
    for axis, dim in sides:
        count = lax.axis_size(axis)
        head = lax.slice_in_dim(cells, 0, width, axis=dim)
        tail = lax.slice_in_dim(cells, cells.shape[dim] - width, cells.shape[dim], axis=dim)
        cells = jnp.concatenate(
            [
                lax.ppermute(tail, axis, [(i, (i + 1) % count) for i in range(count)]),
                cells,
                lax.ppermute(head, axis, [((i + 1) % count, i) for i in range(count)]),
            ],
            axis=dim,
        )
    return cells


def from_behind(value, axis, steps):
    count = lax.axis_size(axis)
    pairs = [(source, (source + steps) % count) for source in range(count)]
    return lax.ppermute(value, axis, pairs)


def invert_newton(matrix):
    order = matrix.shape[0]
    identity = np.eye(order)
    scale_one = np.max(np.sum(np.abs(matrix), axis=0))
    scale_inf = np.max(np.sum(np.abs(matrix), axis=1))
    approx = matrix.T / (scale_one * scale_inf)
    for turn_index in range(NEWTON_TURNS):
        approx = approx @ (2.0 * identity - matrix @ approx)
    return approx


def wall_table(points):
    intervals = points - 1
    cheb_nodes = np.cos(np.pi * np.arange(points) / intervals)
    weights = np.ones(points)
    weights[0] = 2.0
    weights[-1] = 2.0
    weights = weights * (-1.0) ** np.arange(points)
    spread = cheb_nodes[:, None] - cheb_nodes[None, :]
    first_deriv = weights[:, None] / weights[None, :] / (spread + np.eye(points))
    first_deriv = first_deriv - np.eye(points) * first_deriv.sum(axis=1)[:, None]
    second = first_deriv @ first_deriv
    interior = np.eye(points - 2) - WALL_COEF * second[1:-1, 1:-1]
    helm_table = np.zeros((points, points))
    helm_table[1:-1, 1:-1] = invert_newton(interior)
    return jnp.asarray(helm_table.T, dtype=jnp.float32)


def advance(padded, velocity, shear, table_t):
    center = padded[:, 2:-2, 2:-2, :]
    fwd2_x = padded[:, 4:, 2:-2, :]
    fwd1_x = padded[:, 3:-1, 2:-2, :]
    back1_x = padded[:, 1:-3, 2:-2, :]
    back2_x = padded[:, :-4, 2:-2, :]
    fwd2_z = padded[:, 2:-2, 4:, :]
    fwd1_z = padded[:, 2:-2, 3:-1, :]
    back1_z = padded[:, 2:-2, 1:-3, :]
    back2_z = padded[:, 2:-2, :-4, :]
    advect = (back2_x - fwd2_x + 8.0 * (fwd1_x - back1_x)) / 12.0
    lap_x = (16.0 * (fwd1_x + back1_x) - (fwd2_x + back2_x) - 30.0 * center) / 12.0
    lap_z = (16.0 * (fwd1_z + back1_z) - (fwd2_z + back2_z) - 30.0 * center) / 12.0
    explicit = center + TIME_STEP * velocity * advect + DIFFUSE * (lap_x + lap_z)
    explicit = jnp.concatenate(
        [explicit[:1], explicit[1:2] - TIME_STEP * shear * center[:1], explicit[2:]], axis=0
    )
    flattened = explicit.reshape(-1, explicit.shape[-1])
    updated = jnp.dot(
        flattened, table_t, precision=lax.Precision.HIGHEST, preferred_element_type=jnp.float32
    )
    return updated.reshape(explicit.shape)


def extend(adjoint, width):
    along_x = with_halo(adjoint, (("gx", 1),), width)
    return with_halo(along_x, (("gz", 2),), width)


def shards(terminal, jump, tangent, base_velocity, base_shear):
    table_t = wall_table(base_velocity.shape[0])
    received = from_behind(terminal, "seg", -1)
    started = received[0] + jump[0]
    direction = tangent[0]
    products = lax.psum(
        (jnp.sum(started * direction), jnp.sum(direction * direction)), ("gx", "gz")
    )
    along_coef = products[0] / (products[1] + EPSILON)
    adjoint = started - along_coef * direction
    for step_index in range(STEPS):
        padded = extend(adjoint, 2)
        adjoint = advance(padded, base_velocity, base_shear, table_t)
    return adjoint[None]


def solution(mesh):
    in_specs = (
        P("seg", None, "gx", "gz", None),
        P("seg", None, "gx", "gz", None),
        P("seg", None, "gx", "gz", None),
        P(),
        P(),
    )
    out_specs = P("seg", None, "gx", "gz", None)
    return jax.shard_map(shards, mesh=mesh, in_specs=in_specs, out_specs=out_specs, check_vma=False)
```

profile of v0, /device:TPU:22, one launch (start us, length us, event | category | flops | bytes accessed | tf_op | source)
XLA Modules:
  0.0 248.8 jit_solution(7663834592041668082)
XLA Ops:
  0.3 73.3 %collective-permute-done = f32[1,3,64,16,256]{4,3,2,1,0:T(8,128)S(1)} collective-permute-done((f32[1,3,64,16,256]{4,3,2,1,0:T(8,128)}, f32[1,3,64,16,256]{4,3,2,1,0:T(8,128)S(1)}, u32[]{:S(2)}, u32[]{:S(2)}) %collective-permute-start) | collective-permute-done | bytes 3145760 | tf_op jit(solution)/shard_map/ppermute | solution.py:34
  73.7 5.4 %fusion.39 = (f32[]{:T(128)}, f32[]{:T(128)}) fusion(f32[1,3,64,16,256]{4,3,2,1,0:T(8,128)} %param.8, f32[1,3,64,16,256]{4,3,2,1,0:T(8,128)S(1)} %collective-permute-done, f32[1,3,64,16,256]{4,3,2,1,0:T(8,128)} %param.7), kind=kLoop, calls=%fused_computation.85 | loop fusion | flops 3932158 | bytes 9437192 | tf_op jit(solution)/shard_map/reduce_sum | solution.py:100
  79.1 58.7 %all-reduce = (f32[]{:T(128)}, f32[]{:T(128)}) all-reduce(f32[]{:T(128)} %get-tuple-element.6, f32[]{:T(128)} %get-tuple-element.5), channel_id=1, replica_groups=mesh['seg'=8,'gx'=2,'gz'=16] {'gx','gz'}, use_global_device_ids=true, to_apply=%region_1.0 | all-reduce | flops 2 | bytes 16 | tf_op jit(solution)/shard_map/psum | solution.py:99
  139.2 4.0 %fusion.40 = f32[3,64,16,256]{3,2,1,0:T(8,128)S(1)} fusion(f32[1,3,64,16,256]{4,3,2,1,0:T(8,128)S(1)} %copy-done, f32[]{:T(128)S(6)} %div.31, f32[1,3,64,16,256]{4,3,2,1,0:T(8,128)} %copy-done.1, f32[1,3,64,16,256]{4,3,2,1,0:T(8,128)} %param.7), kind=kLoop, calls=%fused_computation.86 | loop fusion | flops 2359296 | bytes 12582916 | tf_op jit(solution)/shard_map/sub | solution.py:103
  143.2 0.8 collective-permute-start.1
  144.0 1.3 collective-permute-start.2
  145.3 2.6 %collective-permute-done.1 = f32[3,2,16,256]{3,2,1,0:T(8,128)S(1)} collective-permute-done((f32[3,2,16,256]{3,2,1,0:T(8,128)S(1)}, f32[3,2,16,256]{3,2,1,0:T(8,128)S(1)}, u32[]{:S(2)}, u32[]{:S(2)}) %collective-permute-start.1) | collective-permute-done | bytes 98336 | tf_op jit(solution)/shard_map/ppermute | solution.py:22
  147.9 1.1 collective-permute-done.2
  149.3 0.5 collective-permute-start.4
  149.8 5.0 %collective-permute-done.3 = f32[3,68,2,256]{3,2,1,0:T(2,128)S(1)} collective-permute-done((f32[3,68,2,256]{3,2,1,0:T(2,128)S(1)}, f32[3,68,2,256]{3,2,1,0:T(2,128)S(1)}, u32[]{:S(2)}, u32[]{:S(2)}) %collective-permute-start.3) | collective-permute-done | bytes 417824 | tf_op jit(solution)/shard_map/ppermute | solution.py:24
  154.8 3.1 %collective-permute-done.4 = f32[3,68,2,256]{3,2,1,0:T(2,128)S(1)} collective-permute-done((f32[3,68,2,256]{3,2,1,0:T(2,128)S(1)}, f32[3,68,2,256]{3,2,1,0:T(2,128)S(1)}, u32[]{:S(2)}, u32[]{:S(2)}) %collective-permute-start.4) | collective-permute-done | bytes 417824 | tf_op jit(solution)/shard_map/ppermute | solution.py:22
  158.0 1.3 pad_maximum_fusion
  159.3 4.1 %fusion.30 = f32[3,64,16,256]{3,2,1,0:T(8,128)} fusion(f32[3,68,18,256]{3,2,1,0:T(8,128)S(1)} %get-tuple-element.22, f32[3,68,18,256]{3,2,1,0:T(8,128)S(1)} %get-tuple-element.21, f32[3,64,16,256]{3,2,1,0:T(8,128)S(1)} %fusion.40, f32[3,2,16,256]{3,2,1,0:T(8,128)S(1)} %collective-permute-done.2, f32[3,2,16,256]{3,2,1,0:T(8,128)S(1)} %collective-permute-done.1, ...), kind=kLoop, calls=%fused_computation.67 | loop fusion | flops 18874368 | bytes 19072000 | tf_op jit(solution)/shard_map/add | solution.py:78
  163.4 2.3 fusion.52
  166.0 0.6 copy-done.2
  166.7 2.6 %fusion.54 = f32[3072,256]{1,0:T(8,128)S(1)} fusion(f32[3072,256]{1,0:T(8,128)S(1)} %bitcast.47, f32[256,256]{1,0:T(8,128)S(1)} %copy-done.2), kind=kOutput, calls=%fused_computation.116 | convolution fusion | flops 2415919104 | bytes 6553600 | tf_op jit(solution)/shard_map/dot_general | solution.py:83
  169.3 1.1 collective-permute-start.5
  170.4 1.1 collective-permute-start.6
  171.4 2.6 %collective-permute-done.5 = f32[3,2,16,256]{3,2,1,0:T(8,128)S(1)} collective-permute-done((f32[3,2,16,256]{3,2,1,0:T(8,128)S(1)}, f32[3,2,16,256]{3,2,1,0:T(8,128)S(1)}, u32[]{:S(2)}, u32[]{:S(2)}) %collective-permute-start.5) | collective-permute-done | bytes 98336 | tf_op jit(solution)/shard_map/ppermute | solution.py:22
  174.0 1.1 collective-permute-done.6
  175.4 0.5 collective-permute-start.8
  176.0 5.0 %collective-permute-done.7 = f32[3,68,2,256]{3,2,1,0:T(2,128)S(1)} collective-permute-done((f32[3,68,2,256]{3,2,1,0:T(2,128)S(1)}, f32[3,68,2,256]{3,2,1,0:T(2,128)S(1)}, u32[]{:S(2)}, u32[]{:S(2)}) %collective-permute-start.7) | collective-permute-done | bytes 417824 | tf_op jit(solution)/shard_map/ppermute | solution.py:24
  181.0 3.1 %collective-permute-done.8 = f32[3,68,2,256]{3,2,1,0:T(2,128)S(1)} collective-permute-done((f32[3,68,2,256]{3,2,1,0:T(2,128)S(1)}, f32[3,68,2,256]{3,2,1,0:T(2,128)S(1)}, u32[]{:S(2)}, u32[]{:S(2)}) %collective-permute-start.8) | collective-permute-done | bytes 417824 | tf_op jit(solution)/shard_map/ppermute | solution.py:22
  184.1 1.3 pad_maximum_fusion.1
  185.4 5.0 %fusion.24 = f32[3,64,16,256]{3,2,1,0:T(8,128)} fusion(f32[3,68,18,256]{3,2,1,0:T(8,128)S(1)} %get-tuple-element.18, f32[3,68,18,256]{3,2,1,0:T(8,128)S(1)} %get-tuple-element.17, f32[3,64,16,256]{3,2,1,0:T(8,128)S(1)} %bitcast.41, f32[3,2,16,256]{3,2,1,0:T(8,128)} %copy-done.3, f32[3,2,16,256]{3,2,1,0:T(8,128)S(1)} %collective-permute-done.5, ...), kind=kLoop, calls=%fused_computation.57 | loop fusion | flops 18874368 | bytes 19072000 | tf_op jit(solution)/shard_map/add | solution.py:78
  190.4 2.3 fusion.50
  193.0 2.6 %fusion.55 = f32[3072,256]{1,0:T(8,128)S(1)} fusion(f32[3072,256]{1,0:T(8,128)S(1)} %bitcast.48, f32[256,256]{1,0:T(8,128)S(1)} %copy-done.2), kind=kOutput, calls=%fused_computation.117 | convolution fusion | flops 2415919104 | bytes 6553600 | tf_op jit(solution)/shard_map/dot_general | solution.py:83
  195.7 1.1 collective-permute-start.10
  196.8 1.1 collective-permute-start.9
  197.8 2.6 %collective-permute-done.10 = f32[3,2,16,256]{3,2,1,0:T(8,128)S(1)} collective-permute-done((f32[3,2,16,256]{3,2,1,0:T(8,128)S(1)}, f32[3,2,16,256]{3,2,1,0:T(8,128)S(1)}, u32[]{:S(2)}, u32[]{:S(2)}) %collective-permute-start.10) | collective-permute-done | bytes 98336 | tf_op jit(solution)/shard_map/ppermute | solution.py:24
  200.4 1.1 collective-permute-done.9
  201.8 0.5 collective-permute-start.12
  202.3 5.0 %collective-permute-done.11 = f32[3,68,2,256]{3,2,1,0:T(2,128)S(1)} collective-permute-done((f32[3,68,2,256]{3,2,1,0:T(2,128)S(1)}, f32[3,68,2,256]{3,2,1,0:T(2,128)S(1)}, u32[]{:S(2)}, u32[]{:S(2)}) %collective-permute-start.11) | collective-permute-done | bytes 417824 | tf_op jit(solution)/shard_map/ppermute | solution.py:24
  207.3 3.1 %collective-permute-done.12 = f32[3,68,2,256]{3,2,1,0:T(2,128)S(1)} collective-permute-done((f32[3,68,2,256]{3,2,1,0:T(2,128)S(1)}, f32[3,68,2,256]{3,2,1,0:T(2,128)S(1)}, u32[]{:S(2)}, u32[]{:S(2)}) %collective-permute-start.12) | collective-permute-done | bytes 417824 | tf_op jit(solution)/shard_map/ppermute | solution.py:22
  210.5 1.3 pad_maximum_fusion.2
  211.8 4.9 %fusion.18 = f32[3,64,16,256]{3,2,1,0:T(8,128)} fusion(f32[3,68,18,256]{3,2,1,0:T(8,128)S(1)} %get-tuple-element.14, f32[3,68,18,256]{3,2,1,0:T(8,128)S(1)} %get-tuple-element.13, f32[3,64,16,256]{3,2,1,0:T(8,128)S(1)} %bitcast.45, f32[3,2,16,256]{3,2,1,0:T(8,128)S(1)} %collective-permute-done.10, f32[3,2,16,256]{3,2,1,0:T(8,128)} %copy-done.4, ...), kind=kLoop, calls=%fused_computation.47 | loop fusion | flops 18874368 | bytes 19072000 | tf_op jit(solution)/shard_map/add | solution.py:78
  216.6 2.3 fusion.48
  219.3 2.6 %fusion.56 = f32[3072,256]{1,0:T(8,128)S(1)} fusion(f32[3072,256]{1,0:T(8,128)S(1)} %bitcast.46, f32[256,256]{1,0:T(8,128)S(1)} %copy-done.2), kind=kOutput, calls=%fused_computation.118 | convolution fusion | flops 2415919104 | bytes 6553600 | tf_op jit(solution)/shard_map/dot_general | solution.py:83
  221.9 1.1 collective-permute-start.13
  223.0 1.0 collective-permute-start.14
  224.1 2.6 %collective-permute-done.13 = f32[3,2,16,256]{3,2,1,0:T(8,128)S(1)} collective-permute-done((f32[3,2,16,256]{3,2,1,0:T(8,128)S(1)}, f32[3,2,16,256]{3,2,1,0:T(8,128)S(1)}, u32[]{:S(2)}, u32[]{:S(2)}) %collective-permute-start.13) | collective-permute-done | bytes 98336 | tf_op jit(solution)/shard_map/ppermute | solution.py:22
  226.7 1.1 collective-permute-done.14
  228.6 5.0 %collective-permute-done.15 = f32[3,68,2,256]{3,2,1,0:T(2,128)S(1)} collective-permute-done((f32[3,68,2,256]{3,2,1,0:T(2,128)S(1)}, f32[3,68,2,256]{3,2,1,0:T(2,128)S(1)}, u32[]{:S(2)}, u32[]{:S(2)}) %collective-permute-start.15) | collective-permute-done | bytes 417824 | tf_op jit(solution)/shard_map/ppermute | solution.py:24
  233.6 3.1 %collective-permute-done.16 = f32[3,68,2,256]{3,2,1,0:T(2,128)S(1)} collective-permute-done((f32[3,68,2,256]{3,2,1,0:T(2,128)S(1)}, f32[3,68,2,256]{3,2,1,0:T(2,128)S(1)}, u32[]{:S(2)}, u32[]{:S(2)}) %collective-permute-start.16) | collective-permute-done | bytes 417824 | tf_op jit(solution)/shard_map/ppermute | solution.py:22
  236.7 1.3 pad_maximum_fusion.3
  238.0 4.1 %fusion.12 = f32[3,64,16,256]{3,2,1,0:T(8,128)} fusion(f32[3,68,18,256]{3,2,1,0:T(8,128)S(1)} %get-tuple-element.10, f32[3,68,18,256]{3,2,1,0:T(8,128)S(1)} %get-tuple-element.9, f32[3,64,16,256]{3,2,1,0:T(8,128)S(1)} %bitcast.37, f32[3,2,16,256]{3,2,1,0:T(8,128)S(1)} %collective-permute-done.14, f32[3,2,16,256]{3,2,1,0:T(8,128)S(1)} %collective-permute-done.13, ...), kind=kLoop, calls=%fused_computation.37 | loop fusion | flops 18874368 | bytes 19072000 | tf_op jit(solution)/shard_map/add | solution.py:78
  242.1 2.4 fusion.46
  244.5 4.3 %fusion.41 = f32[1,3,64,16,256]{4,3,2,1,0:T(8,128)} fusion(f32[256,256,1,1]{1,0,3,2:T(8,128)S(1)} %copy-done.5, f32[1,64,16,256]{3,2,1,0:T(8,128)S(1)} %get-tuple-element.26, f32[1,64,16,256]{3,2,1,0:T(8,128)S(1)} %get-tuple-element.27, f32[1,64,16,256]{3,2,1,0:T(8,128)S(1)} %get-tuple-element.25), kind=kOutput, calls=%fused_computation.87 | convolution fusion | flops 2417491968 | bytes 6553600 | tf_op jit(solution)/shard_map/dot_general | solution.py:83
  (37 shorter events, 3.3 us)
Async XLA Ops:
  0.0 139.1 %copy-start = (f32[1,3,64,16,256]{4,3,2,1,0:T(8,128)S(1)}, f32[1,3,64,16,256]{4,3,2,1,0:T(8,128)}, u32[]{:S(2)}) copy-start(f32[1,3,64,16,256]{4,3,2,1,0:T(8,128)} %param.8) | copy-start | bytes 9437188
  0.0 73.7 %collective-permute-start = (f32[1,3,64,16,256]{4,3,2,1,0:T(8,128)}, f32[1,3,64,16,256]{4,3,2,1,0:T(8,128)S(1)}, u32[]{:S(2)}, u32[]{:S(2)}) collective-permute-start(f32[1,3,64,16,256]{4,3,2,1,0:T(8,128)} %param.6), channel_id=1, source_target_pairs={{0,224},{32,0},{64,32},{96,64},{128,96},{160,128},{192,160},{224,1... | collective-permute-start | bytes 9437192 | tf_op jit(solution)/shard_map/ppermute | solution.py:34
  73.7 5.4 %copy-start.1 = (f32[1,3,64,16,256]{4,3,2,1,0:T(8,128)}, f32[1,3,64,16,256]{4,3,2,1,0:T(8,128)S(1)}, u32[]{:S(2)}) copy-start(f32[1,3,64,16,256]{4,3,2,1,0:T(8,128)S(1)} %collective-permute-done) | copy-start | bytes 9437188
  143.2 6.6 %copy-start.6 = (f32[256]{0:T(256)S(1)}, f32[256]{0:T(256)}, u32[]{:S(2)}) copy-start(f32[256]{0:T(256)} %param.9) | copy-start | bytes 3076
  143.2 6.6 %copy-start.7 = (f32[256]{0:T(256)S(1)}, f32[256]{0:T(256)}, u32[]{:S(2)}) copy-start(f32[256]{0:T(256)} %param.10) | copy-start | bytes 3076
  143.2 4.7 %collective-permute-start.1 = (f32[3,2,16,256]{3,2,1,0:T(8,128)S(1)}, f32[3,2,16,256]{3,2,1,0:T(8,128)S(1)}, u32[]{:S(2)}, u32[]{:S(2)}) collective-permute-start(f32[3,2,16,256]{3,2,1,0:T(8,128)S(1)} %get-tuple-element.43), channel_id=1, source_target_pairs={{0,16},{16,0},{1,17},{17,1},{2,18},{18,2},{3,19},{19,3},{4,20},{20... | collective-permute-start | bytes 294920 | tf_op jit(solution)/shard_map/ppermute | solution.py:22
  144.0 4.9 %collective-permute-start.2 = (f32[3,2,16,256]{3,2,1,0:T(8,128)S(1)}, f32[3,2,16,256]{3,2,1,0:T(8,128)S(1)}, u32[]{:S(2)}, u32[]{:S(2)}) collective-permute-start(f32[3,2,16,256]{3,2,1,0:T(8,128)S(1)} %get-tuple-element.44), channel_id=1, source_target_pairs={{16,0},{0,16},{17,1},{1,17},{18,2},{2,18},{19,3},{3,19},{20,4},{4,... | collective-permute-start | bytes 294920 | tf_op jit(solution)/shard_map/ppermute | solution.py:24
  149.3 5.6 %collective-permute-start.3 = (f32[3,68,2,256]{3,2,1,0:T(2,128)S(1)}, f32[3,68,2,256]{3,2,1,0:T(2,128)S(1)}, u32[]{:S(2)}, u32[]{:S(2)}) collective-permute-start(f32[3,68,2,256]{3,2,1,0:T(2,128)S(1)} %get-tuple-element.23), channel_id=1, source_target_pairs={{1,0},{2,1},{3,2},{4,3},{5,4},{6,5},{7,6},{8,7},{9,8},{10,9},{11,1... | collective-permute-start | bytes 1253384 | tf_op jit(solution)/shard_map/ppermute | solution.py:24
  149.3 8.7 %collective-permute-start.4 = (f32[3,68,2,256]{3,2,1,0:T(2,128)S(1)}, f32[3,68,2,256]{3,2,1,0:T(2,128)S(1)}, u32[]{:S(2)}, u32[]{:S(2)}) collective-permute-start(f32[3,68,2,256]{3,2,1,0:T(2,128)S(1)} %get-tuple-element.24), channel_id=1, source_target_pairs={{0,1},{1,2},{2,3},{3,4},{4,5},{5,6},{6,7},{7,8},{8,9},{9,10},{10,1... | collective-permute-start | bytes 1253384 | tf_op jit(solution)/shard_map/ppermute | solution.py:22
  165.7 1.0 copy-start.2
  169.3 4.7 %collective-permute-start.5 = (f32[3,2,16,256]{3,2,1,0:T(8,128)S(1)}, f32[3,2,16,256]{3,2,1,0:T(8,128)S(1)}, u32[]{:S(2)}, u32[]{:S(2)}) collective-permute-start(f32[3,2,16,256]{3,2,1,0:T(8,128)S(1)} %get-tuple-element.38), channel_id=1, source_target_pairs={{0,16},{16,0},{1,17},{17,1},{2,18},{18,2},{3,19},{19,3},{4,20},{20... | collective-permute-start | bytes 294920 | tf_op jit(solution)/shard_map/ppermute | solution.py:22
  170.4 4.7 %collective-permute-start.6 = (f32[3,2,16,256]{3,2,1,0:T(8,128)S(1)}, f32[3,2,16,256]{3,2,1,0:T(8,128)S(1)}, u32[]{:S(2)}, u32[]{:S(2)}) collective-permute-start(f32[3,2,16,256]{3,2,1,0:T(8,128)S(1)} %get-tuple-element.39), channel_id=1, source_target_pairs={{16,0},{0,16},{17,1},{1,17},{18,2},{2,18},{19,3},{3,19},{20,4},{4,... | collective-permute-start | bytes 294920 | tf_op jit(solution)/shard_map/ppermute | solution.py:24
  175.1 10.3 %copy-start.3 = (f32[3,2,16,256]{3,2,1,0:T(8,128)}, f32[3,2,16,256]{3,2,1,0:T(8,128)S(1)}, u32[]{:S(2)}) copy-start(f32[3,2,16,256]{3,2,1,0:T(8,128)S(1)} %collective-permute-done.6) | copy-start | bytes 294916
  175.4 5.6 %collective-permute-start.7 = (f32[3,68,2,256]{3,2,1,0:T(2,128)S(1)}, f32[3,68,2,256]{3,2,1,0:T(2,128)S(1)}, u32[]{:S(2)}, u32[]{:S(2)}) collective-permute-start(f32[3,68,2,256]{3,2,1,0:T(2,128)S(1)} %get-tuple-element.19), channel_id=1, source_target_pairs={{1,0},{2,1},{3,2},{4,3},{5,4},{6,5},{7,6},{8,7},{9,8},{10,9},{11,1... | collective-permute-start | bytes 1253384 | tf_op jit(solution)/shard_map/ppermute | solution.py:24
  175.4 8.7 %collective-permute-start.8 = (f32[3,68,2,256]{3,2,1,0:T(2,128)S(1)}, f32[3,68,2,256]{3,2,1,0:T(2,128)S(1)}, u32[]{:S(2)}, u32[]{:S(2)}) collective-permute-start(f32[3,68,2,256]{3,2,1,0:T(2,128)S(1)} %get-tuple-element.20), channel_id=1, source_target_pairs={{0,1},{1,2},{2,3},{3,4},{4,5},{5,6},{6,7},{7,8},{8,9},{9,10},{10,1... | collective-permute-start | bytes 1253384 | tf_op jit(solution)/shard_map/ppermute | solution.py:22
  195.7 4.7 %collective-permute-start.10 = (f32[3,2,16,256]{3,2,1,0:T(8,128)S(1)}, f32[3,2,16,256]{3,2,1,0:T(8,128)S(1)}, u32[]{:S(2)}, u32[]{:S(2)}) collective-permute-start(f32[3,2,16,256]{3,2,1,0:T(8,128)S(1)} %get-tuple-element.34), channel_id=1, source_target_pairs={{16,0},{0,16},{17,1},{1,17},{18,2},{2,18},{19,3},{3,19},{20,4},{4,... | collective-permute-start | bytes 294920 | tf_op jit(solution)/shard_map/ppermute | solution.py:24
  196.8 4.7 %collective-permute-start.9 = (f32[3,2,16,256]{3,2,1,0:T(8,128)S(1)}, f32[3,2,16,256]{3,2,1,0:T(8,128)S(1)}, u32[]{:S(2)}, u32[]{:S(2)}) collective-permute-start(f32[3,2,16,256]{3,2,1,0:T(8,128)S(1)} %get-tuple-element.33), channel_id=1, source_target_pairs={{0,16},{16,0},{1,17},{17,1},{2,18},{18,2},{3,19},{19,3},{4,20},{20... | collective-permute-start | bytes 294920 | tf_op jit(solution)/shard_map/ppermute | solution.py:22
  201.4 10.3 %copy-start.4 = (f32[3,2,16,256]{3,2,1,0:T(8,128)}, f32[3,2,16,256]{3,2,1,0:T(8,128)S(1)}, u32[]{:S(2)}) copy-start(f32[3,2,16,256]{3,2,1,0:T(8,128)S(1)} %collective-permute-done.9) | copy-start | bytes 294916
  201.7 5.6 %collective-permute-start.11 = (f32[3,68,2,256]{3,2,1,0:T(2,128)S(1)}, f32[3,68,2,256]{3,2,1,0:T(2,128)S(1)}, u32[]{:S(2)}, u32[]{:S(2)}) collective-permute-start(f32[3,68,2,256]{3,2,1,0:T(2,128)S(1)} %get-tuple-element.15), channel_id=1, source_target_pairs={{1,0},{2,1},{3,2},{4,3},{5,4},{6,5},{7,6},{8,7},{9,8},{10,9},{11,1... | collective-permute-start | bytes 1253384 | tf_op jit(solution)/shard_map/ppermute | solution.py:24
  201.8 8.7 %collective-permute-start.12 = (f32[3,68,2,256]{3,2,1,0:T(2,128)S(1)}, f32[3,68,2,256]{3,2,1,0:T(2,128)S(1)}, u32[]{:S(2)}, u32[]{:S(2)}) collective-permute-start(f32[3,68,2,256]{3,2,1,0:T(2,128)S(1)} %get-tuple-element.16), channel_id=1, source_target_pairs={{0,1},{1,2},{2,3},{3,4},{4,5},{5,6},{6,7},{7,8},{8,9},{9,10},{10,1... | collective-permute-start | bytes 1253384 | tf_op jit(solution)/shard_map/ppermute | solution.py:22
  221.9 4.7 %collective-permute-start.13 = (f32[3,2,16,256]{3,2,1,0:T(8,128)S(1)}, f32[3,2,16,256]{3,2,1,0:T(8,128)S(1)}, u32[]{:S(2)}, u32[]{:S(2)}) collective-permute-start(f32[3,2,16,256]{3,2,1,0:T(8,128)S(1)} %get-tuple-element.28), channel_id=1, source_target_pairs={{0,16},{16,0},{1,17},{17,1},{2,18},{18,2},{3,19},{19,3},{4,20},{20... | collective-permute-start | bytes 294920 | tf_op jit(solution)/shard_map/ppermute | solution.py:22
  223.0 4.7 %collective-permute-start.14 = (f32[3,2,16,256]{3,2,1,0:T(8,128)S(1)}, f32[3,2,16,256]{3,2,1,0:T(8,128)S(1)}, u32[]{:S(2)}, u32[]{:S(2)}) collective-permute-start(f32[3,2,16,256]{3,2,1,0:T(8,128)S(1)} %get-tuple-element.29), channel_id=1, source_target_pairs={{16,0},{0,16},{17,1},{1,17},{18,2},{2,18},{19,3},{3,19},{20,4},{4,... | collective-permute-start | bytes 294920 | tf_op jit(solution)/shard_map/ppermute | solution.py:24
  228.0 5.6 %collective-permute-start.15 = (f32[3,68,2,256]{3,2,1,0:T(2,128)S(1)}, f32[3,68,2,256]{3,2,1,0:T(2,128)S(1)}, u32[]{:S(2)}, u32[]{:S(2)}) collective-permute-start(f32[3,68,2,256]{3,2,1,0:T(2,128)S(1)} %get-tuple-element.11), channel_id=1, source_target_pairs={{1,0},{2,1},{3,2},{4,3},{5,4},{6,5},{7,6},{8,7},{9,8},{10,9},{11,1... | collective-permute-start | bytes 1253384 | tf_op jit(solution)/shard_map/ppermute | solution.py:24
  228.0 8.7 %collective-permute-start.16 = (f32[3,68,2,256]{3,2,1,0:T(2,128)S(1)}, f32[3,68,2,256]{3,2,1,0:T(2,128)S(1)}, u32[]{:S(2)}, u32[]{:S(2)}) collective-permute-start(f32[3,68,2,256]{3,2,1,0:T(2,128)S(1)} %get-tuple-element.12), channel_id=1, source_target_pairs={{0,1},{1,2},{2,3},{3,4},{4,5},{5,6},{6,7},{7,8},{8,9},{9,10},{10,1... | collective-permute-start | bytes 1253384 | tf_op jit(solution)/shard_map/ppermute | solution.py:22
  242.1 2.4 copy-start.5
where the time goes:
time: 249 us
  waiting for transfers between devices  120 us (48%)
  blocking collectives  58.7 us (24%)
  other arithmetic  44.1 us (18%)
  matrix products  12.1 us (5%)
  starting transfers between devices  10.8 us (4%)
    ppermute x1, waiting for transfers between devices, from_behind(): return lax.ppermute(value, axis, pairs)  73.3 us
    psum x1, blocking collectives, shards(): lax.psum((jnp.sum(started * direction), jnp.sum(direction * direction)),...  58.7 us
    ppermute x8, waiting for transfers between devices, with_halo(): lax.ppermute(head, axis, [((i + 1) % count, i) for i in range(count)])  25.7 us
    ppermute x8, waiting for transfers between devices, with_halo(): lax.ppermute(tail, axis, [(i, (i + 1) % count) for i in range(count)])  21.4 us
    add x4, other arithmetic, advance(): center + TIME_STEP * velocity * advect + DIFFUSE * (lap_x + lap_z)  18 us
    dot_general x4, matrix products, advance(): jnp.dot(flattened, table_t, precision=lax.Precision.HIGHEST, preferred_el...  12.1 us
    slice x4, other arithmetic, advance(): explicit[:1]  9.38 us
    ppermute x8, starting transfers between devices, with_halo(): lax.ppermute(tail, axis, [(i, (i + 1) % count) for i in range(count)])  5.99 us
  transfers between devices with their start and end apart: 17, of which 17 were waited for; matrix products, arithmetic and copies ran while one was open for 0% of the time, Pallas kernels for 0%

commit v1 on v0

--- a/solution.py
+++ b/solution.py
@@ -96,9 +96,9 @@
     received = from_behind(terminal, "seg", -1)
     started = received[0] + jump[0]
     direction = tangent[0]
-    products = lax.psum(
-        (jnp.sum(started * direction), jnp.sum(direction * direction)), ("gx", "gz")
-    )
+    products = (jnp.sum(started * direction), jnp.sum(direction * direction))
+    for k0 in ("gx", "gz"):
+        products = lax.psum(products, k0)
     along_coef = products[0] / (products[1] + EPSILON)
     adjoint = started - along_coef * direction
     for step_index in range(STEPS):

time: 249 us -> 226 us (0.908)
  blocking collectives: 58.7 us -> 33.1 us
  waiting for transfers between devices: 120 us -> 123 us
    psum x1 -> x2, blocking collectives: 58.7 us -> 33.1 us  [shards(): products = lax.psum(products, k0)]
where the time goes in v1:
time: 226 us; the launch traced here: 225 us
  waiting for transfers between devices  123 us (54%)
  other arithmetic  44.1 us (20%)
  blocking collectives  33.1 us (15%)
  matrix products  12.1 us (5%)
  starting transfers between devices  10.9 us (5%)
    ppermute x1, waiting for transfers between devices, from_behind(): return lax.ppermute(value, axis, pairs)  73.3 us
    psum x2, blocking collectives, shards(): products = lax.psum(products, k0)  33.1 us
    ppermute x8, waiting for transfers between devices, with_halo(): lax.ppermute(head, axis, [((i + 1) % count, i) for i in range(count)])  27.3 us
    ppermute x8, waiting for transfers between devices, with_halo(): lax.ppermute(tail, axis, [(i, (i + 1) % count) for i in range(count)])  22.3 us
    add x4, other arithmetic, advance(): center + TIME_STEP * velocity * advect + DIFFUSE * (lap_x + lap_z)  18 us
    dot_general x4, matrix products, advance(): jnp.dot(flattened, table_t, precision=lax.Precision.HIGHEST, preferred_el...  12.1 us
    slice x4, other arithmetic, advance(): explicit[:1]  9.38 us
    ppermute x8, starting transfers between devices, with_halo(): lax.ppermute(tail, axis, [(i, (i + 1) % count) for i in range(count)])  5.83 us
  transfers between devices with their start and end apart: 17, of which 17 were waited for; matrix products, arithmetic and copies ran while one was open for 0% of the time, Pallas kernels for 0%

profile of v1, /device:TPU:22, one launch (start us, length us, event | category | flops | bytes accessed | tf_op | source)
XLA Modules:
  0.0 225.5 jit_solution(18263741179743924742)
XLA Ops:
  0.3 73.3 %collective-permute-done = f32[1,3,64,16,256]{4,3,2,1,0:T(8,128)S(1)} collective-permute-done((f32[1,3,64,16,256]{4,3,2,1,0:T(8,128)}, f32[1,3,64,16,256]{4,3,2,1,0:T(8,128)S(1)}, u32[]{:S(2)}, u32[]{:S(2)}) %collective-permute-start) | collective-permute-done | bytes 3145760 | tf_op jit(solution)/shard_map/ppermute | solution.py:34
  73.7 5.4 %fusion.39 = (f32[]{:T(128)}, f32[]{:T(128)}) fusion(f32[1,3,64,16,256]{4,3,2,1,0:T(8,128)} %param.8, f32[1,3,64,16,256]{4,3,2,1,0:T(8,128)S(1)} %collective-permute-done, f32[1,3,64,16,256]{4,3,2,1,0:T(8,128)} %param.7), kind=kLoop, calls=%fused_computation.85 | loop fusion | flops 3932158 | bytes 9437192 | tf_op jit(solution)/shard_map/reduce_sum | solution.py:99
  79.1 5.6 %all-reduce.1 = (f32[]{:T(128)}, f32[]{:T(128)}) all-reduce(f32[]{:T(128)} %get-tuple-element.6, f32[]{:T(128)} %get-tuple-element.5), channel_id=1, replica_groups=mesh['seg'=8,'gx'=2,'gz'=16] {'gx'}, use_global_device_ids=true, to_apply=%region_1.0 | all-reduce | flops 2 | bytes 16 | tf_op jit(solution)/shard_map/psum | solution.py:101
  84.7 27.5 %all-reduce = (f32[]{:T(128)}, f32[]{:T(128)}) all-reduce(f32[]{:T(128)} %get-tuple-element.9, f32[]{:T(128)} %get-tuple-element.10), channel_id=1, replica_groups=mesh['seg'=8,'gx'=2,'gz'=16] {'gz'}, use_global_device_ids=true, to_apply=%region_2.0 | all-reduce | flops 2 | bytes 16 | tf_op jit(solution)/shard_map/psum | solution.py:101
  113.4 4.0 %fusion.40 = f32[3,64,16,256]{3,2,1,0:T(8,128)S(1)} fusion(f32[1,3,64,16,256]{4,3,2,1,0:T(8,128)S(1)} %copy-done, f32[]{:T(128)S(6)} %div.31, f32[1,3,64,16,256]{4,3,2,1,0:T(8,128)} %copy-done.1, f32[1,3,64,16,256]{4,3,2,1,0:T(8,128)} %param.7), kind=kLoop, calls=%fused_computation.86 | loop fusion | flops 2359296 | bytes 12582916 | tf_op jit(solution)/shard_map/sub | solution.py:103
  117.4 1.4 collective-permute-start.1
  118.8 0.7 collective-permute-start.2
  119.5 3.3 %collective-permute-done.1 = f32[3,2,16,256]{3,2,1,0:T(8,128)S(1)} collective-permute-done((f32[3,2,16,256]{3,2,1,0:T(8,128)S(1)}, f32[3,2,16,256]{3,2,1,0:T(8,128)S(1)}, u32[]{:S(2)}, u32[]{:S(2)}) %collective-permute-start.1) | collective-permute-done | bytes 98336 | tf_op jit(solution)/shard_map/ppermute | solution.py:22
  122.9 1.1 collective-permute-done.2
  124.3 0.5 collective-permute-start.4
  124.8 5.0 %collective-permute-done.3 = f32[3,68,2,256]{3,2,1,0:T(2,128)S(1)} collective-permute-done((f32[3,68,2,256]{3,2,1,0:T(2,128)S(1)}, f32[3,68,2,256]{3,2,1,0:T(2,128)S(1)}, u32[]{:S(2)}, u32[]{:S(2)}) %collective-permute-start.3) | collective-permute-done | bytes 417824 | tf_op jit(solution)/shard_map/ppermute | solution.py:24
  129.8 3.1 %collective-permute-done.4 = f32[3,68,2,256]{3,2,1,0:T(2,128)S(1)} collective-permute-done((f32[3,68,2,256]{3,2,1,0:T(2,128)S(1)}, f32[3,68,2,256]{3,2,1,0:T(2,128)S(1)}, u32[]{:S(2)}, u32[]{:S(2)}) %collective-permute-start.4) | collective-permute-done | bytes 417824 | tf_op jit(solution)/shard_map/ppermute | solution.py:22
  132.9 1.3 pad_maximum_fusion
  134.3 4.1 %fusion.30 = f32[3,64,16,256]{3,2,1,0:T(8,128)} fusion(f32[3,68,18,256]{3,2,1,0:T(8,128)S(1)} %get-tuple-element.24, f32[3,68,18,256]{3,2,1,0:T(8,128)S(1)} %get-tuple-element.23, f32[3,64,16,256]{3,2,1,0:T(8,128)S(1)} %fusion.40, f32[3,2,16,256]{3,2,1,0:T(8,128)S(1)} %collective-permute-done.2, f32[3,2,16,256]{3,2,1,0:T(8,128)S(1)} %collective-permute-done.1, ...), kind=kLoop, calls=%fused_computation.67 | loop fusion | flops 18874368 | bytes 19072000 | tf_op jit(solution)/shard_map/add | solution.py:78
  138.3 2.3 %fusion.52 = (f32[1,64,16,256]{3,2,1,0:T(8,128)S(1)}, f32[1,64,16,256]{3,2,1,0:T(8,128)S(1)}, f32[1,64,16,256]{3,2,1,0:T(8,128)S(1)}) fusion(f32[3,64,16,256]{3,2,1,0:T(8,128)} %fusion.30, f32[3,64,16,256]{3,2,1,0:T(8,128)S(1)} %fusion.40, f32[256]{0:T(256)S(1)} %broadcast_multiply_fusion), kind=kLoop, calls=%fused_computation.114 | loop fusion | flops 524288 | bytes 7341056 | tf_op jit(solution)/shard_map/slice | solution.py:80
  141.0 0.6 copy-done.2
  141.6 2.6 %fusion.54 = f32[3072,256]{1,0:T(8,128)S(1)} fusion(f32[3072,256]{1,0:T(8,128)S(1)} %bitcast.47, f32[256,256]{1,0:T(8,128)S(1)} %copy-done.2), kind=kOutput, calls=%fused_computation.116 | convolution fusion | flops 2415919104 | bytes 6553600 | tf_op jit(solution)/shard_map/dot_general | solution.py:83
  144.3 1.4 collective-permute-start.5
  145.7 0.7 collective-permute-start.6
  146.4 2.6 %collective-permute-done.5 = f32[3,2,16,256]{3,2,1,0:T(8,128)S(1)} collective-permute-done((f32[3,2,16,256]{3,2,1,0:T(8,128)S(1)}, f32[3,2,16,256]{3,2,1,0:T(8,128)S(1)}, u32[]{:S(2)}, u32[]{:S(2)}) %collective-permute-start.5) | collective-permute-done | bytes 98336 | tf_op jit(solution)/shard_map/ppermute | solution.py:22
  149.0 1.3 collective-permute-done.6
  151.2 5.3 %collective-permute-done.7 = f32[3,68,2,256]{3,2,1,0:T(2,128)S(1)} collective-permute-done((f32[3,68,2,256]{3,2,1,0:T(2,128)S(1)}, f32[3,68,2,256]{3,2,1,0:T(2,128)S(1)}, u32[]{:S(2)}, u32[]{:S(2)}) %collective-permute-start.7) | collective-permute-done | bytes 417824 | tf_op jit(solution)/shard_map/ppermute | solution.py:24
  156.5 3.1 %collective-permute-done.8 = f32[3,68,2,256]{3,2,1,0:T(2,128)S(1)} collective-permute-done((f32[3,68,2,256]{3,2,1,0:T(2,128)S(1)}, f32[3,68,2,256]{3,2,1,0:T(2,128)S(1)}, u32[]{:S(2)}, u32[]{:S(2)}) %collective-permute-start.8) | collective-permute-done | bytes 417824 | tf_op jit(solution)/shard_map/ppermute | solution.py:22
  159.6 1.3 pad_maximum_fusion.1
  160.9 5.0 %fusion.24 = f32[3,64,16,256]{3,2,1,0:T(8,128)} fusion(f32[3,68,18,256]{3,2,1,0:T(8,128)S(1)} %get-tuple-element.20, f32[3,68,18,256]{3,2,1,0:T(8,128)S(1)} %get-tuple-element.19, f32[3,64,16,256]{3,2,1,0:T(8,128)S(1)} %bitcast.41, f32[3,2,16,256]{3,2,1,0:T(8,128)} %copy-done.3, f32[3,2,16,256]{3,2,1,0:T(8,128)S(1)} %collective-permute-done.5, ...), kind=kLoop, calls=%fused_computation.57 | loop fusion | flops 18874368 | bytes 19072000 | tf_op jit(solution)/shard_map/add | solution.py:78
  165.9 2.3 %fusion.50 = (f32[1,64,16,256]{3,2,1,0:T(8,128)S(1)}, f32[1,64,16,256]{3,2,1,0:T(8,128)S(1)}, f32[1,64,16,256]{3,2,1,0:T(8,128)S(1)}) fusion(f32[3,64,16,256]{3,2,1,0:T(8,128)} %fusion.24, f32[1,64,16,256]{3,2,1,0:T(8,128)S(1)} %bitcast.50, f32[256]{0:T(256)S(1)} %broadcast_multiply_fusion), kind=kLoop, calls=%fused_computation.112 | loop fusion | flops 524288 | bytes 7341056 | tf_op jit(solution)/shard_map/slice | solution.py:80
  168.5 2.6 %fusion.55 = f32[3072,256]{1,0:T(8,128)S(1)} fusion(f32[3072,256]{1,0:T(8,128)S(1)} %bitcast.48, f32[256,256]{1,0:T(8,128)S(1)} %copy-done.2), kind=kOutput, calls=%fused_computation.117 | convolution fusion | flops 2415919104 | bytes 6553600 | tf_op jit(solution)/shard_map/dot_general | solution.py:83
  171.2 1.4 collective-permute-start.10
  172.6 0.7 collective-permute-start.9
  173.3 2.6 %collective-permute-done.10 = f32[3,2,16,256]{3,2,1,0:T(8,128)S(1)} collective-permute-done((f32[3,2,16,256]{3,2,1,0:T(8,128)S(1)}, f32[3,2,16,256]{3,2,1,0:T(8,128)S(1)}, u32[]{:S(2)}, u32[]{:S(2)}) %collective-permute-start.10) | collective-permute-done | bytes 98336 | tf_op jit(solution)/shard_map/ppermute | solution.py:24
  175.9 1.3 collective-permute-done.9
  177.5 0.4 collective-permute-start.11
  178.1 5.4 %collective-permute-done.11 = f32[3,68,2,256]{3,2,1,0:T(2,128)S(1)} collective-permute-done((f32[3,68,2,256]{3,2,1,0:T(2,128)S(1)}, f32[3,68,2,256]{3,2,1,0:T(2,128)S(1)}, u32[]{:S(2)}, u32[]{:S(2)}) %collective-permute-start.11) | collective-permute-done | bytes 417824 | tf_op jit(solution)/shard_map/ppermute | solution.py:24
  183.4 3.1 %collective-permute-done.12 = f32[3,68,2,256]{3,2,1,0:T(2,128)S(1)} collective-permute-done((f32[3,68,2,256]{3,2,1,0:T(2,128)S(1)}, f32[3,68,2,256]{3,2,1,0:T(2,128)S(1)}, u32[]{:S(2)}, u32[]{:S(2)}) %collective-permute-start.12) | collective-permute-done | bytes 417824 | tf_op jit(solution)/shard_map/ppermute | solution.py:22
  186.6 1.3 pad_maximum_fusion.2
  187.9 4.9 %fusion.18 = f32[3,64,16,256]{3,2,1,0:T(8,128)} fusion(f32[3,68,18,256]{3,2,1,0:T(8,128)S(1)} %get-tuple-element.16, f32[3,68,18,256]{3,2,1,0:T(8,128)S(1)} %get-tuple-element.15, f32[3,64,16,256]{3,2,1,0:T(8,128)S(1)} %bitcast.45, f32[3,2,16,256]{3,2,1,0:T(8,128)S(1)} %collective-permute-done.10, f32[3,2,16,256]{3,2,1,0:T(8,128)} %copy-done.4, ...), kind=kLoop, calls=%fused_computation.47 | loop fusion | flops 18874368 | bytes 19072000 | tf_op jit(solution)/shard_map/add | solution.py:78
  192.7 2.3 %fusion.48 = (f32[1,64,16,256]{3,2,1,0:T(8,128)S(1)}, f32[1,64,16,256]{3,2,1,0:T(8,128)S(1)}, f32[1,64,16,256]{3,2,1,0:T(8,128)S(1)}) fusion(f32[3,64,16,256]{3,2,1,0:T(8,128)} %fusion.18, f32[1,64,16,256]{3,2,1,0:T(8,128)S(1)} %bitcast.51, f32[256]{0:T(256)S(1)} %broadcast_multiply_fusion), kind=kLoop, calls=%fused_computation.110 | loop fusion | flops 524288 | bytes 7341056 | tf_op jit(solution)/shard_map/slice | solution.py:80
  195.4 2.6 %fusion.56 = f32[3072,256]{1,0:T(8,128)S(1)} fusion(f32[3072,256]{1,0:T(8,128)S(1)} %bitcast.46, f32[256,256]{1,0:T(8,128)S(1)} %copy-done.2), kind=kOutput, calls=%fused_computation.118 | convolution fusion | flops 2415919104 | bytes 6553600 | tf_op jit(solution)/shard_map/dot_general | solution.py:83
  198.1 1.4 collective-permute-start.13
  199.5 0.7 collective-permute-start.14
  200.2 2.6 %collective-permute-done.13 = f32[3,2,16,256]{3,2,1,0:T(8,128)S(1)} collective-permute-done((f32[3,2,16,256]{3,2,1,0:T(8,128)S(1)}, f32[3,2,16,256]{3,2,1,0:T(8,128)S(1)}, u32[]{:S(2)}, u32[]{:S(2)}) %collective-permute-start.13) | collective-permute-done | bytes 98336 | tf_op jit(solution)/shard_map/ppermute | solution.py:22
  202.8 1.3 collective-permute-done.14
  205.0 5.3 %collective-permute-done.15 = f32[3,68,2,256]{3,2,1,0:T(2,128)S(1)} collective-permute-done((f32[3,68,2,256]{3,2,1,0:T(2,128)S(1)}, f32[3,68,2,256]{3,2,1,0:T(2,128)S(1)}, u32[]{:S(2)}, u32[]{:S(2)}) %collective-permute-start.15) | collective-permute-done | bytes 417824 | tf_op jit(solution)/shard_map/ppermute | solution.py:24
  210.3 3.1 %collective-permute-done.16 = f32[3,68,2,256]{3,2,1,0:T(2,128)S(1)} collective-permute-done((f32[3,68,2,256]{3,2,1,0:T(2,128)S(1)}, f32[3,68,2,256]{3,2,1,0:T(2,128)S(1)}, u32[]{:S(2)}, u32[]{:S(2)}) %collective-permute-start.16) | collective-permute-done | bytes 417824 | tf_op jit(solution)/shard_map/ppermute | solution.py:22
  213.4 1.3 pad_maximum_fusion.3
  214.7 4.1 %fusion.12 = f32[3,64,16,256]{3,2,1,0:T(8,128)} fusion(f32[3,68,18,256]{3,2,1,0:T(8,128)S(1)} %get-tuple-element.12, f32[3,68,18,256]{3,2,1,0:T(8,128)S(1)} %get-tuple-element.11, f32[3,64,16,256]{3,2,1,0:T(8,128)S(1)} %bitcast.37, f32[3,2,16,256]{3,2,1,0:T(8,128)S(1)} %collective-permute-done.14, f32[3,2,16,256]{3,2,1,0:T(8,128)S(1)} %collective-permute-done.13, ...), kind=kLoop, calls=%fused_computation.37 | loop fusion | flops 18874368 | bytes 19072000 | tf_op jit(solution)/shard_map/add | solution.py:78
  218.8 2.4 %fusion.46 = (f32[1,64,16,256]{3,2,1,0:T(8,128)S(1)}, f32[1,64,16,256]{3,2,1,0:T(8,128)S(1)}, f32[1,64,16,256]{3,2,1,0:T(8,128)S(1)}) fusion(f32[3,64,16,256]{3,2,1,0:T(8,128)} %fusion.12, f32[1,64,16,256]{3,2,1,0:T(8,128)S(1)} %bitcast.49, f32[256]{0:T(256)S(1)} %broadcast_multiply_fusion), kind=kLoop, calls=%fused_computation.108 | loop fusion | flops 524288 | bytes 7341056 | tf_op jit(solution)/shard_map/slice | solution.py:80
  221.2 4.3 %fusion.41 = f32[1,3,64,16,256]{4,3,2,1,0:T(8,128)} fusion(f32[256,256,1,1]{1,0,3,2:T(8,128)S(1)} %copy-done.5, f32[1,64,16,256]{3,2,1,0:T(8,128)S(1)} %get-tuple-element.28, f32[1,64,16,256]{3,2,1,0:T(8,128)S(1)} %get-tuple-element.29, f32[1,64,16,256]{3,2,1,0:T(8,128)S(1)} %get-tuple-element.27), kind=kOutput, calls=%fused_computation.87 | convolution fusion | flops 2417491968 | bytes 6553600 | tf_op jit(solution)/shard_map/dot_general | solution.py:83
  (38 shorter events, 3.9 us)
Async XLA Ops:
  0.0 113.4 %copy-start = (f32[1,3,64,16,256]{4,3,2,1,0:T(8,128)S(1)}, f32[1,3,64,16,256]{4,3,2,1,0:T(8,128)}, u32[]{:S(2)}) copy-start(f32[1,3,64,16,256]{4,3,2,1,0:T(8,128)} %param.8) | copy-start | bytes 9437188
  0.0 73.7 %collective-permute-start = (f32[1,3,64,16,256]{4,3,2,1,0:T(8,128)}, f32[1,3,64,16,256]{4,3,2,1,0:T(8,128)S(1)}, u32[]{:S(2)}, u32[]{:S(2)}) collective-permute-start(f32[1,3,64,16,256]{4,3,2,1,0:T(8,128)} %param.6), channel_id=1, source_target_pairs={{0,224},{32,0},{64,32},{96,64},{128,96},{160,128},{192,160},{224,1... | collective-permute-start | bytes 9437192 | tf_op jit(solution)/shard_map/ppermute | solution.py:34
  73.7 5.4 %copy-start.1 = (f32[1,3,64,16,256]{4,3,2,1,0:T(8,128)}, f32[1,3,64,16,256]{4,3,2,1,0:T(8,128)S(1)}, u32[]{:S(2)}) copy-start(f32[1,3,64,16,256]{4,3,2,1,0:T(8,128)S(1)} %collective-permute-done) | copy-start | bytes 9437188
  117.4 7.4 %copy-start.6 = (f32[256]{0:T(256)S(1)}, f32[256]{0:T(256)}, u32[]{:S(2)}) copy-start(f32[256]{0:T(256)} %param.9) | copy-start | bytes 3076
  117.4 7.4 %copy-start.7 = (f32[256]{0:T(256)S(1)}, f32[256]{0:T(256)}, u32[]{:S(2)}) copy-start(f32[256]{0:T(256)} %param.10) | copy-start | bytes 3076
  117.4 5.5 %collective-permute-start.1 = (f32[3,2,16,256]{3,2,1,0:T(8,128)S(1)}, f32[3,2,16,256]{3,2,1,0:T(8,128)S(1)}, u32[]{:S(2)}, u32[]{:S(2)}) collective-permute-start(f32[3,2,16,256]{3,2,1,0:T(8,128)S(1)} %get-tuple-element.45), channel_id=1, source_target_pairs={{0,16},{16,0},{1,17},{17,1},{2,18},{18,2},{3,19},{19,3},{4,20},{20... | collective-permute-start | bytes 294920 | tf_op jit(solution)/shard_map/ppermute | solution.py:22
  118.8 5.1 %collective-permute-start.2 = (f32[3,2,16,256]{3,2,1,0:T(8,128)S(1)}, f32[3,2,16,256]{3,2,1,0:T(8,128)S(1)}, u32[]{:S(2)}, u32[]{:S(2)}) collective-permute-start(f32[3,2,16,256]{3,2,1,0:T(8,128)S(1)} %get-tuple-element.46), channel_id=1, source_target_pairs={{16,0},{0,16},{17,1},{1,17},{18,2},{2,18},{19,3},{3,19},{20,4},{4,... | collective-permute-start | bytes 294920 | tf_op jit(solution)/shard_map/ppermute | solution.py:24
  124.2 5.6 %collective-permute-start.3 = (f32[3,68,2,256]{3,2,1,0:T(2,128)S(1)}, f32[3,68,2,256]{3,2,1,0:T(2,128)S(1)}, u32[]{:S(2)}, u32[]{:S(2)}) collective-permute-start(f32[3,68,2,256]{3,2,1,0:T(2,128)S(1)} %get-tuple-element.25), channel_id=1, source_target_pairs={{1,0},{2,1},{3,2},{4,3},{5,4},{6,5},{7,6},{8,7},{9,8},{10,9},{11,1... | collective-permute-start | bytes 1253384 | tf_op jit(solution)/shard_map/ppermute | solution.py:24
  124.3 8.7 %collective-permute-start.4 = (f32[3,68,2,256]{3,2,1,0:T(2,128)S(1)}, f32[3,68,2,256]{3,2,1,0:T(2,128)S(1)}, u32[]{:S(2)}, u32[]{:S(2)}) collective-permute-start(f32[3,68,2,256]{3,2,1,0:T(2,128)S(1)} %get-tuple-element.26), channel_id=1, source_target_pairs={{0,1},{1,2},{2,3},{3,4},{4,5},{5,6},{6,7},{7,8},{8,9},{9,10},{10,1... | collective-permute-start | bytes 1253384 | tf_op jit(solution)/shard_map/ppermute | solution.py:22
  140.7 1.0 copy-start.2
  144.3 4.7 %collective-permute-start.5 = (f32[3,2,16,256]{3,2,1,0:T(8,128)S(1)}, f32[3,2,16,256]{3,2,1,0:T(8,128)S(1)}, u32[]{:S(2)}, u32[]{:S(2)}) collective-permute-start(f32[3,2,16,256]{3,2,1,0:T(8,128)S(1)} %get-tuple-element.40), channel_id=1, source_target_pairs={{0,16},{16,0},{1,17},{17,1},{2,18},{18,2},{3,19},{19,3},{4,20},{20... | collective-permute-start | bytes 294920 | tf_op jit(solution)/shard_map/ppermute | solution.py:22
  145.7 4.6 %collective-permute-start.6 = (f32[3,2,16,256]{3,2,1,0:T(8,128)S(1)}, f32[3,2,16,256]{3,2,1,0:T(8,128)S(1)}, u32[]{:S(2)}, u32[]{:S(2)}) collective-permute-start(f32[3,2,16,256]{3,2,1,0:T(8,128)S(1)} %get-tuple-element.41), channel_id=1, source_target_pairs={{16,0},{0,16},{17,1},{1,17},{18,2},{2,18},{19,3},{3,19},{20,4},{4,... | collective-permute-start | bytes 294920 | tf_op jit(solution)/shard_map/ppermute | solution.py:24
  150.3 10.6 %copy-start.3 = (f32[3,2,16,256]{3,2,1,0:T(8,128)}, f32[3,2,16,256]{3,2,1,0:T(8,128)S(1)}, u32[]{:S(2)}) copy-start(f32[3,2,16,256]{3,2,1,0:T(8,128)S(1)} %collective-permute-done.6) | copy-start | bytes 294916
  150.6 5.9 %collective-permute-start.7 = (f32[3,68,2,256]{3,2,1,0:T(2,128)S(1)}, f32[3,68,2,256]{3,2,1,0:T(2,128)S(1)}, u32[]{:S(2)}, u32[]{:S(2)}) collective-permute-start(f32[3,68,2,256]{3,2,1,0:T(2,128)S(1)} %get-tuple-element.21), channel_id=1, source_target_pairs={{1,0},{2,1},{3,2},{4,3},{5,4},{6,5},{7,6},{8,7},{9,8},{10,9},{11,1... | collective-permute-start | bytes 1253384 | tf_op jit(solution)/shard_map/ppermute | solution.py:24
  150.9 8.7 %collective-permute-start.8 = (f32[3,68,2,256]{3,2,1,0:T(2,128)S(1)}, f32[3,68,2,256]{3,2,1,0:T(2,128)S(1)}, u32[]{:S(2)}, u32[]{:S(2)}) collective-permute-start(f32[3,68,2,256]{3,2,1,0:T(2,128)S(1)} %get-tuple-element.22), channel_id=1, source_target_pairs={{0,1},{1,2},{2,3},{3,4},{4,5},{5,6},{6,7},{7,8},{8,9},{9,10},{10,1... | collective-permute-start | bytes 1253384 | tf_op jit(solution)/shard_map/ppermute | solution.py:22
  171.2 4.7 %collective-permute-start.10 = (f32[3,2,16,256]{3,2,1,0:T(8,128)S(1)}, f32[3,2,16,256]{3,2,1,0:T(8,128)S(1)}, u32[]{:S(2)}, u32[]{:S(2)}) collective-permute-start(f32[3,2,16,256]{3,2,1,0:T(8,128)S(1)} %get-tuple-element.36), channel_id=1, source_target_pairs={{16,0},{0,16},{17,1},{1,17},{18,2},{2,18},{19,3},{3,19},{20,4},{4,... | collective-permute-start | bytes 294920 | tf_op jit(solution)/shard_map/ppermute | solution.py:24
  172.6 4.6 %collective-permute-start.9 = (f32[3,2,16,256]{3,2,1,0:T(8,128)S(1)}, f32[3,2,16,256]{3,2,1,0:T(8,128)S(1)}, u32[]{:S(2)}, u32[]{:S(2)}) collective-permute-start(f32[3,2,16,256]{3,2,1,0:T(8,128)S(1)} %get-tuple-element.35), channel_id=1, source_target_pairs={{0,16},{16,0},{1,17},{17,1},{2,18},{18,2},{3,19},{19,3},{4,20},{20... | collective-permute-start | bytes 294920 | tf_op jit(solution)/shard_map/ppermute | solution.py:22
  177.2 10.7 %copy-start.4 = (f32[3,2,16,256]{3,2,1,0:T(8,128)}, f32[3,2,16,256]{3,2,1,0:T(8,128)S(1)}, u32[]{:S(2)}) copy-start(f32[3,2,16,256]{3,2,1,0:T(8,128)S(1)} %collective-permute-done.9) | copy-start | bytes 294916
  177.5 5.9 %collective-permute-start.11 = (f32[3,68,2,256]{3,2,1,0:T(2,128)S(1)}, f32[3,68,2,256]{3,2,1,0:T(2,128)S(1)}, u32[]{:S(2)}, u32[]{:S(2)}) collective-permute-start(f32[3,68,2,256]{3,2,1,0:T(2,128)S(1)} %get-tuple-element.17), channel_id=1, source_target_pairs={{1,0},{2,1},{3,2},{4,3},{5,4},{6,5},{7,6},{8,7},{9,8},{10,9},{11,1... | collective-permute-start | bytes 1253384 | tf_op jit(solution)/shard_map/ppermute | solution.py:24
  177.9 8.7 %collective-permute-start.12 = (f32[3,68,2,256]{3,2,1,0:T(2,128)S(1)}, f32[3,68,2,256]{3,2,1,0:T(2,128)S(1)}, u32[]{:S(2)}, u32[]{:S(2)}) collective-permute-start(f32[3,68,2,256]{3,2,1,0:T(2,128)S(1)} %get-tuple-element.18), channel_id=1, source_target_pairs={{0,1},{1,2},{2,3},{3,4},{4,5},{5,6},{6,7},{7,8},{8,9},{9,10},{10,1... | collective-permute-start | bytes 1253384 | tf_op jit(solution)/shard_map/ppermute | solution.py:22
  198.1 4.7 %collective-permute-start.13 = (f32[3,2,16,256]{3,2,1,0:T(8,128)S(1)}, f32[3,2,16,256]{3,2,1,0:T(8,128)S(1)}, u32[]{:S(2)}, u32[]{:S(2)}) collective-permute-start(f32[3,2,16,256]{3,2,1,0:T(8,128)S(1)} %get-tuple-element.30), channel_id=1, source_target_pairs={{0,16},{16,0},{1,17},{17,1},{2,18},{18,2},{3,19},{19,3},{4,20},{20... | collective-permute-start | bytes 294920 | tf_op jit(solution)/shard_map/ppermute | solution.py:22
  199.5 4.6 %collective-permute-start.14 = (f32[3,2,16,256]{3,2,1,0:T(8,128)S(1)}, f32[3,2,16,256]{3,2,1,0:T(8,128)S(1)}, u32[]{:S(2)}, u32[]{:S(2)}) collective-permute-start(f32[3,2,16,256]{3,2,1,0:T(8,128)S(1)} %get-tuple-element.31), channel_id=1, source_target_pairs={{16,0},{0,16},{17,1},{1,17},{18,2},{2,18},{19,3},{3,19},{20,4},{4,... | collective-permute-start | bytes 294920 | tf_op jit(solution)/shard_map/ppermute | solution.py:24
  204.4 5.9 %collective-permute-start.15 = (f32[3,68,2,256]{3,2,1,0:T(2,128)S(1)}, f32[3,68,2,256]{3,2,1,0:T(2,128)S(1)}, u32[]{:S(2)}, u32[]{:S(2)}) collective-permute-start(f32[3,68,2,256]{3,2,1,0:T(2,128)S(1)} %get-tuple-element.13), channel_id=1, source_target_pairs={{1,0},{2,1},{3,2},{4,3},{5,4},{6,5},{7,6},{8,7},{9,8},{10,9},{11,1... | collective-permute-start | bytes 1253384 | tf_op jit(solution)/shard_map/ppermute | solution.py:24
  204.7 8.7 %collective-permute-start.16 = (f32[3,68,2,256]{3,2,1,0:T(2,128)S(1)}, f32[3,68,2,256]{3,2,1,0:T(2,128)S(1)}, u32[]{:S(2)}, u32[]{:S(2)}) collective-permute-start(f32[3,68,2,256]{3,2,1,0:T(2,128)S(1)} %get-tuple-element.14), channel_id=1, source_target_pairs={{0,1},{1,2},{2,3},{3,4},{4,5},{5,6},{6,7},{7,8},{8,9},{9,10},{10,1... | collective-permute-start | bytes 1253384 | tf_op jit(solution)/shard_map/ppermute | solution.py:22
  218.8 2.4 %copy-start.5 = (f32[256,256,1,1]{1,0,3,2:T(8,128)S(1)}, f32[256,256,1,1]{1,0,3,2:T(8,128)}, u32[]{:S(2)}) copy-start(f32[256,256,1,1]{1,0,3,2:T(8,128)} %constant.40) | copy-start | bytes 786436
